TPU v7x, 512 devices: a whole 4x4x16 slice. The times are simulated.
512 devices in a mesh: dp: 16 (over z), pipe: 4 (over x), tensor: 8 (over y, core).
Axes of the slice: x: 4, y: 4, z: 16, core: 2. Of those that a mesh axis runs over, the one named last changes fastest.
Arguments:
- tokens: bfloat16 [16384, 8192], P('dp', ('pipe', 'tensor')), may hold values from -6 to 6
- key_value_weight: bfloat16 [8192, 2048], P(('pipe', 'tensor')), may hold values from -0.0625 to 0.0625
- adapter_down: bfloat16 [96, 8192, 128], P(None, ('pipe', 'tensor', 'dp')), may hold values from -0.0625 to 0.0625
- adapter_up: bfloat16 [96, 64, 2048], P(None, 'dp'), may hold values from -0.75 to 0.75
- tenant_of_block: int32 [128], replicated, may hold values from 0 to 95
- slot_of_tenant: int32 [96], replicated, may hold values from 0 to 95, each once
- cotangent: bfloat16 [16384, 2048], P(('dp', 'pipe', 'tensor')), may hold values from -1.5 to 1.5
Outputs:
- key_value: bfloat16 [16384, 2048], P(('dp', 'pipe', 'tensor'))
- input_grad: bfloat16 [16384, 8192], P('dp', ('pipe', 'tensor'))
- grad_a: float32 [96, 8192, 128], P(None, ('pipe', 'tensor', 'dp'))
- grad_b: float32 [96, 64, 2048], P(None, 'dp', ('pipe', 'tensor'))
Inputs may be any that keep to these rules, and one draw needn't show every extreme that they name: `slot_of_tenant`: each slot holds exactly one tenant.
All inputs are finite; a program needn't handle non-finite values.
Results may differ from a plain program's by a relative error of at most 0.017.
Values may be sent and summed in bfloat16 or wider, within the bound.
A program may use at most 64 MiB of HBM per device.

v0:
```python
import jax
import jax.numpy as jnp
from jax import lax
from jax.sharding import PartitionSpec as P

KEY_WIDTH = 1024
ADAPTER_RANK = 64
BLOCK = 128


def body(
    tokens, key_value_weight, adapter_down, adapter_up, tenant_of_block, slot_of_tenant, cotangent
):
    data_count = lax.axis_size("dp")
    group_count = lax.axis_size(("pipe", "tensor"))
    my_group = lax.axis_index(("pipe", "tensor"))
    tok_dev, feature_count = tokens.shape
    blocks_dev = tok_dev // BLOCK
    row_count = tok_dev // group_count
    tenant_list = slot_of_tenant.shape[0]
    all_blocks = tenant_of_block.shape[0]
    tenant_ids = lax.broadcasted_iota(jnp.int32, (all_blocks, tenant_list), 1)
    slot_of_block = jnp.sum(
        jnp.where(tenant_of_block[:, None] == tenant_ids, slot_of_tenant[None, :], 0), axis=1
    )
    slot_match = slot_of_block[:, None] == tenant_ids
    down_rows = adapter_down.shape[1]
    a_send = jnp.dot(
        slot_match.astype(jnp.bfloat16),
        adapter_down.reshape(tenant_list, down_rows * 2 * ADAPTER_RANK),
        preferred_element_type=jnp.float32,
    )
    a_send = a_send.astype(jnp.bfloat16).reshape(all_blocks, down_rows, 2 * ADAPTER_RANK)
    own_block = my_group * row_count // BLOCK
    own_slots = lax.dynamic_index_in_dim(
        slot_of_block.reshape(data_count, blocks_dev), own_block, 1, False
    )
    owner_choice = (
        own_slots[:, None] == lax.broadcasted_iota(jnp.int32, (data_count, tenant_list), 1)
    ).astype(jnp.bfloat16)
    up_rows = adapter_up.shape[1]
    b_send = jnp.dot(
        owner_choice,
        adapter_up.reshape(tenant_list, up_rows * 2 * KEY_WIDTH),
        preferred_element_type=jnp.float32,
    )
    b_send = b_send.astype(jnp.bfloat16).reshape(data_count, up_rows, 2 * KEY_WIDTH)
    down_blocks, b_own = (
        lax.all_to_all(a_send, "dp", split_axis=0, concat_axis=1, tiled=True),
        lax.all_to_all(b_send, "dp", split_axis=0, concat_axis=1, tiled=True),
    )
    b_own = b_own[0]
    tok_blocks = tokens.reshape(blocks_dev, BLOCK, feature_count)
    low_part = jnp.einsum(
        "bif,bfr->bir", tok_blocks, down_blocks, preferred_element_type=jnp.float32
    ).reshape(tok_dev, 2 * ADAPTER_RANK)
    low_all = lax.psum(low_part.astype(jnp.bfloat16), ("pipe", "tensor"))
    base_out = lax.psum_scatter(
        jnp.dot(tokens, key_value_weight, preferred_element_type=jnp.float32).astype(jnp.bfloat16),
        ("pipe", "tensor"),
        scatter_dimension=0,
        tiled=True,
    ).astype(jnp.float32)
    low_rows = lax.dynamic_slice_in_dim(low_all, my_group * row_count, row_count, 0)
    lowrank = jnp.concatenate(
        [
            jnp.dot(
                low_rows[:, :ADAPTER_RANK], b_own[:, :KEY_WIDTH], preferred_element_type=jnp.float32
            ),
            jnp.dot(
                low_rows[:, ADAPTER_RANK:], b_own[:, KEY_WIDTH:], preferred_element_type=jnp.float32
            ),
        ],
        axis=1,
    )
    key_value = (base_out + lowrank).astype(jnp.bfloat16)
    contract_last = (((1,), (1,)), ((), ()))
    grad_rows = jnp.concatenate(
        [
            lax.dot_general(
                cotangent[:, :KEY_WIDTH],
                b_own[:, :KEY_WIDTH],
                contract_last,
                preferred_element_type=jnp.float32,
            ),
            lax.dot_general(
                cotangent[:, KEY_WIDTH:],
                b_own[:, KEY_WIDTH:],
                contract_last,
                preferred_element_type=jnp.float32,
            ),
        ],
        axis=1,
    )
    grad_rows = grad_rows.astype(jnp.bfloat16)
    cot_all, grad_low = (
        lax.all_gather(cotangent, ("pipe", "tensor"), axis=0, tiled=True),
        lax.all_gather(grad_rows, ("pipe", "tensor"), axis=0, tiled=True),
    )
    grad_blocks = grad_low.reshape(blocks_dev, BLOCK, 2 * ADAPTER_RANK)
    input_grad = lax.dot_general(
        cot_all, key_value_weight, contract_last, preferred_element_type=jnp.float32
    )
    input_grad = input_grad + jnp.einsum(
        "bir,bfr->bif", grad_blocks, down_blocks, preferred_element_type=jnp.float32
    ).reshape(tok_dev, feature_count)
    input_grad = input_grad.astype(jnp.bfloat16)
    grad_a_part = jnp.einsum(
        "bif,bir->bfr", tok_blocks, grad_blocks, preferred_element_type=jnp.float32
    )
    col_count = 2 * KEY_WIDTH // group_count
    col_start = my_group * col_count
    half_index = col_start // KEY_WIDTH
    low_half = lax.dynamic_slice_in_dim(
        low_all, half_index * ADAPTER_RANK, ADAPTER_RANK, 1
    ).reshape(blocks_dev, BLOCK, ADAPTER_RANK)
    cot_cols = lax.dynamic_slice_in_dim(cot_all, col_start, col_count, 1).reshape(
        blocks_dev, BLOCK, col_count
    )
    grad_b_part = jnp.einsum("bir,bic->brc", low_half, cot_cols, preferred_element_type=jnp.float32)
    grad_a_recv, grad_b_recv = (
        lax.all_to_all(
            grad_a_part.astype(jnp.bfloat16), "dp", split_axis=1, concat_axis=0, tiled=True
        ).astype(grad_a_part.dtype),
        lax.all_to_all(
            grad_b_part.astype(jnp.bfloat16), "dp", split_axis=1, concat_axis=0, tiled=True
        ).astype(grad_b_part.dtype),
    )
    slot_weight = slot_match.astype(jnp.float32)
    grad_a = jnp.einsum(
        "bt,bx->tx",
        slot_weight,
        grad_a_recv.reshape(all_blocks, down_rows * 2 * ADAPTER_RANK),
        precision=lax.Precision.HIGHEST,
    )
    grad_a = grad_a.reshape(tenant_list, down_rows, 2 * ADAPTER_RANK)
    grad_b = jnp.einsum(
        "bt,bx->tx",
        slot_weight,
        grad_b_recv.reshape(all_blocks, grad_b_recv.shape[1] * col_count),
        precision=lax.Precision.HIGHEST,
    )
    grad_b = grad_b.reshape(tenant_list, grad_b_recv.shape[1], col_count)
    return (key_value, input_grad, grad_a, grad_b)


def solution(mesh):
    placed = (
        P("dp", ("pipe", "tensor")),
        P(("pipe", "tensor"), None),
        P(None, ("pipe", "tensor", "dp"), None),
        P(None, "dp", None),
        P(),
        P(),
        P(("dp", "pipe", "tensor"), None),
    )
    return jax.shard_map(
        body,
        mesh=mesh,
        in_specs=placed,
        out_specs=(
            P(("dp", "pipe", "tensor"), None),
            P("dp", ("pipe", "tensor")),
            P(None, ("pipe", "tensor", "dp"), None),
            P(None, "dp", ("pipe", "tensor")),
        ),
        check_vma=False,
    )
```

profile of v0, /device:TPU:2, one launch (start us, length us, event | category | flops | bytes accessed | tf_op | source)
XLA Modules:
  0.0 395.1 jit_solution(17106891758424243477)
XLA Ops:
  7.2 0.0 copy-start
  7.2 0.0 copy-start.1
  7.2 0.0 all-reduce.2.cloned.1.call-start
  7.2 0.9 select_reduce_fusion
  8.1 1.3 fusion.2
  9.5 0.1 copy.60
  9.6 44.1 %all_to_all.57 = bf16[128,16,128]{2,1,0:T(8,128)(2,1)S(1)} all-to-all(bf16[128,16,128]{2,1,0:T(8,128)(2,1)S(1)} %bitcast.78), channel_id=1, replica_groups=mesh['dp'=16,'pipe'=4,'tensor'=8] {'dp'}, dimensions={0} | all-to-all | bytes 1048576 | tf_op jit(solution)/shard_map/all_to_all | solution.py:49
  53.7 0.0 copy-start.2
  53.7 0.8 copy-done.2
  54.5 0.0 copy-done.1
  54.5 0.3 convolution_convert_fusion.4
  54.8 0.9 copy.41
  55.6 0.0 all-reduce.2.cloned.1.call-update
  55.7 0.0 reduce-scatter.2.cloned.1.call-start
  55.7 0.0 copy-done
  55.7 3.2 convolution_convert_fusion.1
  59.0 0.0 reduce-scatter.2.cloned.1.call-update
  59.0 0.0 copy-start.5
  59.0 0.0 all-gather.2.cloned.1.call-start
  59.1 0.7 all-gather.2.cloned.1.call-update
  59.8 0.1 reshape.62
  59.8 2.4 copy.61
  62.3 0.2 dynamic-slice_reduce_fusion
  62.5 0.4 convolution_convert_fusion
  62.8 0.0 copy-start.3
  62.9 0.2 reshape.64
  63.0 24.5 %all_to_all.58 = bf16[16,4,2048]{2,1,0:T(4,128)(2,1)S(1)} all-to-all(bf16[16,4,2048]{2,1,0:T(4,128)(2,1)S(1)} %reshape.64), channel_id=1, replica_groups=mesh['dp'=16,'pipe'=4,'tensor'=8] {'dp'}, dimensions={0} | all-to-all | bytes 524288 | tf_op jit(solution)/shard_map/all_to_all | solution.py:50
  87.5 0.1 squeeze.5
  87.6 0.0 copy-done.5
  87.6 0.0 copy-start.4
  87.6 0.1 fusion.3
  87.8 0.2 fusion.4
  87.9 0.4 copy-done.4
  88.3 0.1 pad_maximum_fusion
  88.4 24.9 %all_gather.7 = bf16[1024,128]{1,0:T(8,128)(2,1)S(1)} all-gather(bf16[32,128]{1,0:T(8,128)(2,1)S(1)} %pad_maximum_fusion), channel_id=1, replica_groups=mesh['dp'=16,'pipe'=4,'tensor'=8] {'pipe','tensor'}, dimensions={0}, use_global_device_ids=true | all-gather | bytes 270336 | tf_op jit(solution)/shard_map/all_gather | solution.py:98
  113.3 0.3 fusion.1
  113.6 1.1 copy.43
  114.7 5.8 %all-to-all-start.2 = ((bf16[8,256,128]{2,0,1:T(8,128)(2,1)}), bf16[8,256,128]{2,0,1:T(8,128)(2,1)S(1)}, u32[]{:S(2)}, u32[]{:S(2)}) async-start(bf16[8,256,128]{2,0,1:T(8,128)(2,1)} %copy.43), calls=%async_computation.3 | async-start | bytes 1048576 | tf_op jit(solution)/shard_map/all_to_all | solution.py:122
  120.5 0.0 copy-done.3
  120.5 0.3 fusion.30
  120.8 63.9 %all-reduce.2.cloned.1.call-done = bf16[1024,128]{0,1:T(8,128)(2,1)} async-done(((bf16[1024,128]{0,1:T(8,128)(2,1)}), bf16[1024,128]{0,1:T(8,128)(2,1)}) %all-reduce.2.cloned.1.call-update) | async-done | bytes 262160 | tf_op jit(solution)/shard_map/psum | solution.py:57
  184.8 1.2 fusion.14
  185.9 1.2 fusion.11
  187.1 0.0 all-to-all-done.2
  187.1 0.3 copy.46
  187.4 0.3 fusion.21
  187.7 1.3 copy.53
  189.1 105.7 %reduce-scatter.2.cloned.1.call-done = bf16[32,2048]{1,0:T(8,128)(2,1)} async-done(((bf16[1024,2048]{1,0:T(8,128)(2,1)}), bf16[32,2048]{1,0:T(8,128)(2,1)}) %reduce-scatter.2.cloned.1.call-update) | async-done | bytes 131088 | tf_op jit(solution)/shard_map/reduce_scatter | solution.py:58
  294.8 1.6 fusion.7
  296.4 62.4 %all-gather.2.cloned.1.call-done = bf16[1024,2048]{1,0:T(8,128)(2,1)} async-done(((bf16[32,2048]{1,0:T(8,128)(2,1)}), bf16[1024,2048]{1,0:T(8,128)(2,1)}) %all-gather.2.cloned.1.call-update) | async-done | bytes 4194320 | tf_op jit(solution)/shard_map/all_gather | solution.py:97
  358.8 1.1 constant_dynamic-slice_fusion
  359.9 1.1 convolution_convert_fusion.5
  361.0 0.1 copy.73
  361.1 0.8 reshape.73
  361.9 12.3 %all-to-all-start.3 = ((bf16[16,2,1024]{2,1,0:T(2,128)(2,1)}), bf16[16,2,1024]{2,1,0:T(2,128)(2,1)S(1)}, u32[]{:S(2)}, u32[]{:S(2)}) async-start(bf16[16,2,1024]{2,1,0:T(2,128)(2,1)} %reshape.73), calls=%async_computation.4 | async-start | bytes 131072 | tf_op jit(solution)/shard_map/all_to_all | solution.py:125
  374.2 4.3 %fusion = bf16[1024,256]{1,0:T(8,128)(2,1)} fusion(f32[1024,256]{1,0:T(8,128)S(1)} %bitcast.81, bf16[1024,2048]{1,0:T(8,128)(2,1)} %all-gather.2.cloned.1.call-done, bf16[256,2048]{1,0:T(8,128)(2,1)S(1)} %copy-done), kind=kOutput, calls=%fused_computation.4 | convolution fusion | flops 1074266112 | bytes 6815744 | tf_op jit(solution)/shard_map/dot_general | solution.py:101
  378.4 8.9 %all-to-all-done.3 = bf16[16,2,1024]{2,1,0:T(2,128)(2,1)S(1)} async-done(((bf16[16,2,1024]{2,1,0:T(2,128)(2,1)}), bf16[16,2,1024]{2,1,0:T(2,128)(2,1)S(1)}, u32[]{:S(2)}, u32[]{:S(2)}) %all-to-all-start.3) | async-done | bytes 65568 | tf_op jit(solution)/shard_map/all_to_all | solution.py:125
  387.3 0.1 reshape.74
  387.5 0.1 copy.72
  387.5 0.1 reshape.70
  387.7 0.1 copy.52
  387.8 0.8 fusion.19
  (1 shorter events, 0.0 us)
Async XLA Ops:
  7.2 48.6 %copy-start = (bf16[256,2048]{1,0:T(8,128)(2,1)S(1)}, bf16[256,2048]{1,0:T(8,128)(2,1)}, u32[]{:S(2)}) copy-start(bf16[256,2048]{1,0:T(8,128)(2,1)} %param.8) | copy-start | bytes 3145732
  7.2 47.3 %copy-start.1 = (bf16[1024,256]{1,0:T(8,128)(2,1)S(1)}, bf16[1024,256]{1,0:T(8,128)(2,1)}, u32[]{:S(2)}) copy-start(bf16[1024,256]{1,0:T(8,128)(2,1)} %param.7) | copy-start | bytes 1572868
  7.2 177.6 %all-reduce.2.cloned.1.call-start = ((), (), s32[]{:S(2)}) async-start(), calls=%async_computation.6 | async-start | bytes 524288 | tf_op jit(solution)/shard_map/psum | solution.py:57
  53.7 0.8 copy-start.2
  55.7 239.1 %reduce-scatter.2.cloned.1.call-start = ((), (), s32[]{:S(2)}) async-start(), calls=%async_computation.5 | async-start | bytes 4325376 | tf_op jit(solution)/shard_map/reduce_scatter | solution.py:58
  59.0 28.6 %copy-start.5 = (bf16[32,2048]{1,0:T(8,128)(2,1)S(1)}, bf16[32,2048]{1,0:T(8,128)(2,1)}, u32[]{:S(2)}) copy-start(bf16[32,2048]{1,0:T(8,128)(2,1)} %param.13) | copy-start | bytes 393220
  59.0 299.8 %all-gather.2.cloned.1.call-start = ((), (), s32[]{:S(2)}) async-start(), calls=%async_computation.7 | async-start | bytes 4325376 | tf_op jit(solution)/shard_map/all_gather | solution.py:97
  62.8 57.7 %copy-start.3 = (bf16[16,8,16,128]{3,2,0,1:T(8,128)(2,1)S(1)}, bf16[16,8,16,128]{3,2,0,1:T(8,128)(2,1)}, u32[]{:S(2)}) copy-start(bf16[16,8,16,128]{3,2,0,1:T(8,128)(2,1)} %copy-done.2) | copy-start | bytes 1572868
  87.6 0.7 copy-start.4
  114.7 72.4 %all-to-all-start.2 = ((bf16[8,256,128]{2,0,1:T(8,128)(2,1)}), bf16[8,256,128]{2,0,1:T(8,128)(2,1)S(1)}, u32[]{:S(2)}, u32[]{:S(2)}) async-start(bf16[8,256,128]{2,0,1:T(8,128)(2,1)} %copy.43), calls=%async_computation.3 | async-start | bytes 1048576 | tf_op jit(solution)/shard_map/all_to_all | solution.py:122
  361.9 25.5 %all-to-all-start.3 = ((bf16[16,2,1024]{2,1,0:T(2,128)(2,1)}), bf16[16,2,1024]{2,1,0:T(2,128)(2,1)S(1)}, u32[]{:S(2)}, u32[]{:S(2)}) async-start(bf16[16,2,1024]{2,1,0:T(2,128)(2,1)} %reshape.73), calls=%async_computation.4 | async-start | bytes 131072 | tf_op jit(solution)/shard_map/all_to_all | solution.py:125
Sparse Core Ops, SparseCore 0:
  55.8 128.9 all-reduce.1
  189.3 105.4 reduce-scatter.1
  297.9 60.8 all-gather.1
where the time goes:
time: 396 us; the launch traced here: 395 us
  waiting for transfers between devices  242 us (61%)
  blocking collectives  93.4 us (24%)
  starting transfers between devices  18.2 us (5%)
  matrix products  15 us (4%)
  between operations  14 us (4%)
  local copies, waits for them, and re-layouts  10.2 us (3%)
    reduce_scatter x1, waiting for transfers between devices, body(): lax.psum_scatter(jnp.dot(tokens, key_value_weight, preferred_element_type...  106 us
    psum x1, waiting for transfers between devices, body(): low_all = lax.psum(low_part.astype(jnp.bfloat16), ('pipe', 'tensor'))  63.9 us
    all_gather x1, waiting for transfers between devices, body(): lax.all_gather(cotangent, ('pipe', 'tensor'), axis=0, tiled=True)  62.4 us
    all_to_all x1, blocking collectives, body(): lax.all_to_all(a_send, 'dp', split_axis=0, concat_axis=1, tiled=True)  44.1 us
    all_gather x1, blocking collectives, body(): lax.all_gather(grad_rows, ('pipe', 'tensor'), axis=0, tiled=True)  24.9 us
    all_to_all x1, blocking collectives, body(): lax.all_to_all(b_send, 'dp', split_axis=0, concat_axis=1, tiled=True)  24.5 us
    all_to_all x1, starting transfers between devices, body(): lax.all_to_all(grad_b_part.astype(jnp.bfloat16), 'dp', split_axis=1, conc...  12.3 us
    all_to_all x1, waiting for transfers between devices, body(): lax.all_to_all(grad_b_part.astype(jnp.bfloat16), 'dp', split_axis=1, conc...  8.89 us
  transfers between devices with their start and end apart: 5, of which 4 were waited for; matrix products, arithmetic and copies ran while one was open for 5% of the time, Pallas kernels for 0%

commit v1 on v0

--- a/solution.py
+++ b/solution.py
@@ -54,7 +54,7 @@
     low_part = jnp.einsum(
         "bif,bfr->bir", tok_blocks, down_blocks, preferred_element_type=jnp.float32
     ).reshape(tok_dev, 2 * ADAPTER_RANK)
-    low_all = lax.psum(low_part.astype(jnp.bfloat16), ("pipe", "tensor"))
+    low_all = lax.psum(lax.psum(low_part.astype(jnp.bfloat16), "tensor"), "pipe")
     base_out = lax.psum_scatter(
         jnp.dot(tokens, key_value_weight, preferred_element_type=jnp.float32).astype(jnp.bfloat16),
         ("pipe", "tensor"),

time: 396 us -> 339 us (0.86)
  waiting for transfers between devices: 242 us -> 179 us
  blocking collectives: 93.4 us -> 97.4 us
    reduce_scatter x1, waiting for transfers between devices: 106 us -> 9.04 us  [body(): lax.psum_scatter(jnp.dot(tokens, key_value_weight, preferred_element_type...]
    all_to_all x1, waiting for transfers between devices: 0.01 us -> 26.6 us  [body(): lax.all_to_all(grad_a_part.astype(jnp.bfloat16), 'dp', split_axis=1, conc...]
    psum x1 -> x2, waiting for transfers between devices: 63.9 us -> 71.5 us  [the longest x1 71.5 us: body(): lax.psum(low_part.astype(jnp.bfloat16), 'tensor')]
    all_to_all x1, blocking collectives: 24.5 us -> 28.5 us  [body(): lax.all_to_all(b_send, 'dp', split_axis=0, concat_axis=1, tiled=True)]
  transfers between devices with their start and end apart: 5 -> 6, of which waited for: 4 -> 5; matrix products, arithmetic and copies ran while one was open for 5% -> 6% of each run, Pallas kernels for 0% -> 0%
where the time goes in v1:
time: 339 us; the launch traced here: 338 us
  waiting for transfers between devices  179 us (53%)
  blocking collectives  97.4 us (29%)
  starting transfers between devices  18.4 us (5%)
  between operations  15.8 us (5%)
  matrix products  15.1 us (4%)
  local copies, waits for them, and re-layouts  10.2 us (3%)
    psum x1, waiting for transfers between devices, body(): lax.psum(low_part.astype(jnp.bfloat16), 'tensor')  71.5 us
    all_gather x1, waiting for transfers between devices, body(): lax.all_gather(cotangent, ('pipe', 'tensor'), axis=0, tiled=True)  62.2 us
    all_to_all x1, blocking collectives, body(): lax.all_to_all(a_send, 'dp', split_axis=0, concat_axis=1, tiled=True)  44.1 us
    all_to_all x1, blocking collectives, body(): lax.all_to_all(b_send, 'dp', split_axis=0, concat_axis=1, tiled=True)  28.5 us
    all_to_all x1, waiting for transfers between devices, body(): lax.all_to_all(grad_a_part.astype(jnp.bfloat16), 'dp', split_axis=1, conc...  26.6 us
    all_gather x1, blocking collectives, body(): lax.all_gather(grad_rows, ('pipe', 'tensor'), axis=0, tiled=True)  24.8 us
    all_to_all x1, starting transfers between devices, body(): lax.all_to_all(grad_b_part.astype(jnp.bfloat16), 'dp', split_axis=1, conc...  12.3 us
    reduce_scatter x1, waiting for transfers between devices, body(): lax.psum_scatter(jnp.dot(tokens, key_value_weight, preferred_element_type...  9.04 us
  transfers between devices with their start and end apart: 6, of which 5 were waited for; matrix products, arithmetic and copies ran while one was open for 6% of the time, Pallas kernels for 0%

profile of v1, /device:TPU:2, one launch (start us, length us, event | category | flops | bytes accessed | tf_op | source)
XLA Modules:
  0.0 338.3 jit_solution(2610249351681543796)
XLA Ops:
  8.0 0.0 copy-start
  8.0 0.0 copy-start.1
  8.0 0.0 all-reduce.3.cloned.1.call-start
  8.1 0.9 select_reduce_fusion
  9.0 1.3 fusion.2
  10.3 0.1 copy.60
  10.4 44.1 %all_to_all.57 = bf16[128,16,128]{2,1,0:T(8,128)(2,1)S(1)} all-to-all(bf16[128,16,128]{2,1,0:T(8,128)(2,1)S(1)} %bitcast.78), channel_id=1, replica_groups=mesh['dp'=16,'pipe'=4,'tensor'=8] {'dp'}, dimensions={0} | all-to-all | bytes 1048576 | tf_op jit(solution)/shard_map/all_to_all | solution.py:49
  54.5 0.0 copy-start.2
  54.5 0.8 copy-done.2
  55.3 0.0 copy-done.1
  55.3 0.3 convolution_convert_fusion.4
  55.6 0.9 copy.41
  56.5 0.0 all-reduce.3.cloned.1.call-update
  56.5 0.0 all-reduce.5.cloned.1.call-start
  56.5 71.5 %all-reduce.3.cloned.1.call-done = bf16[1024,128]{0,1:T(8,128)(2,1)} async-done(((bf16[1024,128]{0,1:T(8,128)(2,1)}), bf16[1024,128]{0,1:T(8,128)(2,1)}) %all-reduce.3.cloned.1.call-update) | async-done | bytes 262160 | tf_op jit(solution)/shard_map/psum | solution.py:57
  128.0 0.0 all-reduce.5.cloned.1.call-update
  128.1 0.0 reduce-scatter.2.cloned.1.call-start
  128.1 0.0 copy-done
  128.1 3.2 convolution_convert_fusion.1
  131.4 0.0 reduce-scatter.2.cloned.1.call-update
  131.4 0.0 copy-start.5
  131.4 0.0 all-gather.2.cloned.1.call-start
  131.4 0.5 all-gather.2.cloned.1.call-update
  132.0 0.1 reshape.62
  132.1 2.4 copy.61
  134.5 0.2 dynamic-slice_reduce_fusion
  134.7 0.4 convolution_convert_fusion
  135.1 0.0 copy-start.3
  135.1 0.2 reshape.64
  135.3 28.5 %all_to_all.58 = bf16[16,4,2048]{2,1,0:T(4,128)(2,1)S(1)} all-to-all(bf16[16,4,2048]{2,1,0:T(4,128)(2,1)S(1)} %reshape.64), channel_id=1, replica_groups=mesh['dp'=16,'pipe'=4,'tensor'=8] {'dp'}, dimensions={0} | all-to-all | bytes 524288 | tf_op jit(solution)/shard_map/all_to_all | solution.py:50
  163.8 0.1 squeeze.5
  163.9 0.0 copy-done.5
  163.9 0.0 copy-start.4
  163.9 0.1 fusion.3
  164.1 0.2 fusion.4
  164.2 0.4 copy-done.4
  164.6 0.1 pad_maximum_fusion
  164.7 24.8 %all_gather.7 = bf16[1024,128]{1,0:T(8,128)(2,1)S(1)} all-gather(bf16[32,128]{1,0:T(8,128)(2,1)S(1)} %pad_maximum_fusion), channel_id=1, replica_groups=mesh['dp'=16,'pipe'=4,'tensor'=8] {'pipe','tensor'}, dimensions={0}, use_global_device_ids=true | all-gather | bytes 270336 | tf_op jit(solution)/shard_map/all_gather | solution.py:98
  189.5 0.3 fusion.1
  189.9 1.1 copy.43
  191.0 6.0 %all-to-all-start.2 = ((bf16[8,256,128]{2,0,1:T(8,128)(2,1)}), bf16[8,256,128]{2,0,1:T(8,128)(2,1)S(1)}, u32[]{:S(2)}, u32[]{:S(2)}) async-start(bf16[8,256,128]{2,0,1:T(8,128)(2,1)} %copy.43), calls=%async_computation.3 | async-start | bytes 1048576 | tf_op jit(solution)/shard_map/all_to_all | solution.py:122
  197.0 0.3 fusion.30
  197.3 0.0 all-reduce.5.cloned.1.call-done
  197.3 1.2 fusion.14
  198.5 1.2 fusion.11
  199.7 26.6 %all-to-all-done.2 = bf16[8,256,128]{2,0,1:T(8,128)(2,1)S(1)} async-done(((bf16[8,256,128]{2,0,1:T(8,128)(2,1)}), bf16[8,256,128]{2,0,1:T(8,128)(2,1)S(1)}, u32[]{:S(2)}, u32[]{:S(2)}) %all-to-all-start.2) | async-done | bytes 524320 | tf_op jit(solution)/shard_map/all_to_all | solution.py:122
  226.3 0.3 copy.46
  226.6 0.3 fusion.21
  226.9 1.3 copy.53
  228.2 9.0 %reduce-scatter.2.cloned.1.call-done = bf16[32,2048]{1,0:T(8,128)(2,1)} async-done(((bf16[1024,2048]{1,0:T(8,128)(2,1)}), bf16[32,2048]{1,0:T(8,128)(2,1)}) %reduce-scatter.2.cloned.1.call-update) | async-done | bytes 131088 | tf_op jit(solution)/shard_map/reduce_scatter | solution.py:58
  237.2 1.6 fusion.7
  238.8 62.2 %all-gather.2.cloned.1.call-done = bf16[1024,2048]{1,0:T(8,128)(2,1)} async-done(((bf16[32,2048]{1,0:T(8,128)(2,1)}), bf16[1024,2048]{1,0:T(8,128)(2,1)}) %all-gather.2.cloned.1.call-update) | async-done | bytes 4194320 | tf_op jit(solution)/shard_map/all_gather | solution.py:97
  301.1 1.1 constant_dynamic-slice_fusion
  302.1 1.1 convolution_convert_fusion.5
  303.3 0.1 copy.73
  303.4 0.8 reshape.73
  304.1 12.3 %all-to-all-start.3 = ((bf16[16,2,1024]{2,1,0:T(2,128)(2,1)}), bf16[16,2,1024]{2,1,0:T(2,128)(2,1)S(1)}, u32[]{:S(2)}, u32[]{:S(2)}) async-start(bf16[16,2,1024]{2,1,0:T(2,128)(2,1)} %reshape.73), calls=%async_computation.4 | async-start | bytes 131072 | tf_op jit(solution)/shard_map/all_to_all | solution.py:125
  316.4 4.3 %fusion = bf16[1024,256]{1,0:T(8,128)(2,1)} fusion(f32[1024,256]{1,0:T(8,128)S(1)} %bitcast.81, bf16[1024,2048]{1,0:T(8,128)(2,1)} %all-gather.2.cloned.1.call-done, bf16[256,2048]{1,0:T(8,128)(2,1)S(1)} %copy-done), kind=kOutput, calls=%fused_computation.4 | convolution fusion | flops 1074266112 | bytes 6815744 | tf_op jit(solution)/shard_map/dot_general | solution.py:101
  320.7 8.9 %all-to-all-done.3 = bf16[16,2,1024]{2,1,0:T(2,128)(2,1)S(1)} async-done(((bf16[16,2,1024]{2,1,0:T(2,128)(2,1)}), bf16[16,2,1024]{2,1,0:T(2,128)(2,1)S(1)}, u32[]{:S(2)}, u32[]{:S(2)}) %all-to-all-start.3) | async-done | bytes 65568 | tf_op jit(solution)/shard_map/all_to_all | solution.py:125
  329.6 0.1 reshape.74
  329.7 0.1 copy.72
  329.8 0.1 reshape.70
  329.9 0.1 copy.52
  330.1 0.8 fusion.19
  (2 shorter events, 0.0 us)
Async XLA Ops:
  8.0 120.1 %copy-start = (bf16[256,2048]{1,0:T(8,128)(2,1)S(1)}, bf16[256,2048]{1,0:T(8,128)(2,1)}, u32[]{:S(2)}) copy-start(bf16[256,2048]{1,0:T(8,128)(2,1)} %param.8) | copy-start | bytes 3145732
  8.0 47.3 %copy-start.1 = (bf16[1024,256]{1,0:T(8,128)(2,1)S(1)}, bf16[1024,256]{1,0:T(8,128)(2,1)}, u32[]{:S(2)}) copy-start(bf16[1024,256]{1,0:T(8,128)(2,1)} %param.7) | copy-start | bytes 1572868
  8.0 120.0 %all-reduce.3.cloned.1.call-start = ((), (), s32[]{:S(2)}) async-start(), calls=%async_computation.6 | async-start | bytes 524288 | tf_op jit(solution)/shard_map/psum | solution.py:57
  54.5 0.8 copy-start.2
  56.5 140.8 %all-reduce.5.cloned.1.call-start = ((), (), s32[]{:S(2)}) async-start(), calls=%async_computation.7 | async-start | bytes 524288 | tf_op jit(solution)/shard_map/psum | solution.py:57
  128.1 109.2 %reduce-scatter.2.cloned.1.call-start = ((), (), s32[]{:S(2)}) async-start(), calls=%async_computation.5 | async-start | bytes 4325376 | tf_op jit(solution)/shard_map/reduce_scatter | solution.py:58
  131.4 32.5 %copy-start.5 = (bf16[32,2048]{1,0:T(8,128)(2,1)S(1)}, bf16[32,2048]{1,0:T(8,128)(2,1)}, u32[]{:S(2)}) copy-start(bf16[32,2048]{1,0:T(8,128)(2,1)} %param.13) | copy-start | bytes 393220
  131.4 169.7 %all-gather.2.cloned.1.call-start = ((), (), s32[]{:S(2)}) async-start(), calls=%async_computation.8 | async-start | bytes 4325376 | tf_op jit(solution)/shard_map/all_gather | solution.py:97
  135.1 61.9 %copy-start.3 = (bf16[16,8,16,128]{3,2,0,1:T(8,128)(2,1)S(1)}, bf16[16,8,16,128]{3,2,0,1:T(8,128)(2,1)}, u32[]{:S(2)}) copy-start(bf16[16,8,16,128]{3,2,0,1:T(8,128)(2,1)} %copy-done.2) | copy-start | bytes 1572868
  163.9 0.7 copy-start.4
  191.0 35.3 %all-to-all-start.2 = ((bf16[8,256,128]{2,0,1:T(8,128)(2,1)}), bf16[8,256,128]{2,0,1:T(8,128)(2,1)S(1)}, u32[]{:S(2)}, u32[]{:S(2)}) async-start(bf16[8,256,128]{2,0,1:T(8,128)(2,1)} %copy.43), calls=%async_computation.3 | async-start | bytes 1048576 | tf_op jit(solution)/shard_map/all_to_all | solution.py:122
  304.1 25.5 %all-to-all-start.3 = ((bf16[16,2,1024]{2,1,0:T(2,128)(2,1)}), bf16[16,2,1024]{2,1,0:T(2,128)(2,1)S(1)}, u32[]{:S(2)}, u32[]{:S(2)}) async-start(bf16[16,2,1024]{2,1,0:T(2,128)(2,1)} %reshape.73), calls=%async_computation.4 | async-start | bytes 131072 | tf_op jit(solution)/shard_map/all_to_all | solution.py:125
Sparse Core Ops, SparseCore 0:
  56.6 71.3 all-reduce.2
  130.3 55.4 all-reduce.4
Sparse Core Ops, SparseCore 1:
  133.0 104.1 reduce-scatter.1
  240.3 60.7 all-gather.1
